TPU v7x, 32 devices: a whole 2x2x4 slice. The times are simulated.
32 devices in a mesh: tile: 8 (over y, x, core), mode: 4 (over z).
Axes of the slice: x: 2, y: 2, z: 4, core: 2. Of those that a mesh axis runs over, the one named last changes fastest.
Arguments:
- object_field: float32 [2, 2, 2048, 384], P(None, None, 'tile'), may hold values from -4 to 4
- probe: float32 [8, 2, 256, 256], P('mode'), may hold values from -4 to 4
- measured: float32 [32, 256, 256], P('tile'), may hold values from 0 to 16
- prop_phase: float32 [256, 256], replicated, may hold values from -3.140625 to 3.140625
- counts: int32 [8], P('tile'), may hold values from 1 to 4, 16 in all
- row_offset: int32 [32], P('tile'), may hold values from 0 to 255
- col_offset: int32 [32], P('tile'), may hold values from 0 to 128
Outputs:
- object_grad: float32 [2, 2, 2048, 384], P(None, None, 'tile')
- probe_grad: float32 [8, 2, 256, 256], P('mode')
Inputs may be any that keep to these rules, and one draw needn't show every extreme that they name: Slot i is live for i % 4 < counts[i // 4]; some tile has all 4 slots live.
All inputs are finite; a program needn't handle non-finite values. No bound on the sum of `counts` on one device may be relied on, other than what follows from the above.
Results may differ from a plain program's by a relative error of at most 0.0003.
Values sent between devices are 32-bit elements; how exact they have to be, the bound alone decides.
A program may use at most 128 MiB of HBM per device.

v0:
```python
import functools
import math

import jax
import jax.numpy as jnp
import numpy as np
from jax import lax
from jax.experimental import pallas as pl
from jax.experimental.pallas import tpu as pltpu
from jax.sharding import PartitionSpec as P

F32 = jnp.float32
BF16 = jnp.bfloat16
MESH = pl.DeviceIdType.MESH
BLOCKS = 8
VMEM_SPEC = pl.BlockSpec(memory_space=pltpu.VMEM)


def shifted(block, axis, distance):
    devices = range(lax.axis_size(axis))
    route = [(i - distance, i) for i in devices if i - distance in devices]
    return lax.ppermute(block, axis, route)


def dft_constants(length):
    half = length // 2
    n, k = np.arange(half)[:, None], np.arange(half)[None, :]
    sides = []
    for side in ("left", "right"):
        for way in range(2):
            for parity in range(2):
                angle = (n * (2 * k + parity) % length) * (2.0 * math.pi / length)
                real = np.cos(angle) / math.sqrt(length)
                imag = (-np.sin(angle) if way == 0 else np.sin(angle)) / math.sqrt(length)
                if (side == "left") == (way == 0):
                    real, imag = real.T, imag.T
                if side == "left":
                    table = np.block([[real, -imag], [imag, real]])
                else:
                    table = np.block([[real, imag], [-imag, real]])
                high = table.astype(BF16)
                sides += [high, (table - high.astype(np.float64)).astype(BF16)]
    return np.stack(sides).reshape(2, 2, 2, 2, length, length)


def build_tables(dft_ref, left_ref, right_ref):
    n = dft_ref.shape[-1]
    for place, low in enumerate((0, 0, 1)):
        for way in range(2):
            for parity in range(2):
                left_ref[way, parity, :, place * n:(place + 1) * n] = dft_ref[0, way, parity, low]
                right_ref[way, parity, place * n:(place + 1) * n, :] = dft_ref[1, way, parity, low]


def split(x, axis):
    high = x.astype(BF16)
    low = (x - high.astype(F32)).astype(BF16)
    return jnp.concatenate([high, low, high], axis=axis)


def one_side(real, imag, product, axis, way):
    half = real.shape[axis] // 2
    first = lambda x: lax.slice_in_dim(x, 0, half, axis=axis)
    second = lambda x: lax.slice_in_dim(x, half, 2 * half, axis=axis)
    join = lambda x, y: jnp.concatenate([x, y], axis=axis)
    if way == 0:
        even = product(split(join(first(real) + second(real), first(imag) + second(imag)), axis), 0)
        odd = product(split(join(first(real) - second(real), first(imag) - second(imag)), axis), 1)
        return join(first(even), first(odd)), join(second(even), second(odd))
    even = product(split(join(first(real), first(imag)), axis), 0)
    odd = product(split(join(second(real), second(imag)), axis), 1)
    total, rest = even + odd, even - odd
    return join(first(total), first(rest)), join(second(total), second(rest))


def transform(real, imag, left_ref, right_ref, way):
    on_left = lambda x, parity: jnp.dot(left_ref[way, parity], x, preferred_element_type=F32)
    on_right = lambda x, parity: jnp.dot(x, right_ref[way, parity], preferred_element_type=F32)
    real, imag = one_side(real, imag, on_left, 0, way)
    return one_side(real, imag, on_right, 1, way)


def to_even_odd(fields):
    n = fields.shape[-1]
    order = np.concatenate([np.arange(0, n, 2), np.arange(1, n, 2)])
    pick = jnp.asarray(np.eye(n, dtype=np.float32)[order])
    high = lax.Precision.HIGHEST
    fields = jnp.einsum("ajk,lk->ajl", fields, pick, precision=high)
    return jnp.einsum("ij,ajl->ail", pick, fields, precision=high)


def times(a, b):
    return a[0] * b[0] - a[1] * b[1], a[0] * b[1] + a[1] * b[0]


def times_conj(a, b):
    return a[0] * b[0] + a[1] * b[1], a[0] * b[1] - a[1] * b[0]


def cut_windows(own_ref, next_ref, ext_ref, window_ref, row, col, first):
    layers, _, tile_rows, columns = own_ref.shape
    width = window_ref.shape[-1]

    @pl.when(first)
    def _():
        ext_ref[:, :, :tile_rows, :] = own_ref[...]
        ext_ref[:, :, tile_rows:, :] = next_ref[...]

    base = pl.multiple_of(row // 8 * 8, 8)
    extra = row - base
    turn = lax.rem(columns - col, columns)
    for layer in range(layers):
        for part in range(2):
            block = ext_ref[layer, part, pl.ds(base, width + 8), :]
            block = pltpu.roll(block, lax.rem(width + 8 - extra, width + 8), 0)[:width]
            window_ref[layer, part] = pltpu.roll(block, turn, 1)[:, :width]


def forward_kernel(count_ref, row_ref, col_ref, own_ref, next_ref, probe_ref, prop_ref, dft_ref,
                   before_ref, far_ref, power_ref, window_out_ref, ext_ref, left_ref, right_ref):
    window_ref = window_out_ref.at[0]
    slot, mode = pl.program_id(0), pl.program_id(1)
    alive = slot < count_ref[0]

    @pl.when((slot == 0) & (mode == 0))
    def _():
        build_tables(dft_ref, left_ref, right_ref)

    @pl.when((mode == 0) & alive)
    def _():
        cut_windows(own_ref, next_ref, ext_ref, window_ref, row_ref[slot], col_ref[slot], slot == 0)

    @pl.when(mode == 0)
    def _():
        power_ref[...] = jnp.zeros_like(power_ref)

    @pl.when(alive)
    def _():
        wave = times((probe_ref[mode, 0], probe_ref[mode, 1]), (window_ref[0, 0], window_ref[0, 1]))
        spectrum = transform(*wave, left_ref, right_ref, 0)
        moved = transform(*times((prop_ref[0], prop_ref[1]), spectrum), left_ref, right_ref, 1)
        before_ref[0, 0, 0] = moved[0]
        before_ref[0, 0, 1] = moved[1]
        wave = times(moved, (window_ref[1, 0], window_ref[1, 1]))
        far = transform(*wave, left_ref, right_ref, 0)
        far_ref[0, 0, 0] = far[0]
        far_ref[0, 0, 1] = far[1]
        power_ref[0] += far[0] * far[0] + far[1] * far[1]


def backward_kernel(count_ref, row_ref, col_ref, probe_ref, prop_ref, dft_ref,
                    before_ref, far_ref, power_ref, measured_ref, window_in_ref,
                    grad_ref, rim_ref, probe_grad_ref, piece_ref, total_ref, left_ref, right_ref, *, modes):
    window_ref = window_in_ref.at[0]
    slot, mode = pl.program_id(0), pl.program_id(1)
    local_modes = pl.num_programs(1)
    alive = slot < count_ref[0]
    layers, _, tile_rows, columns = grad_ref.shape
    width = piece_ref.shape[-1]

    @pl.when((slot == 0) & (mode == 0))
    def _():
        build_tables(dft_ref, left_ref, right_ref)
        total_ref[...] = jnp.zeros_like(total_ref)
        probe_grad_ref[...] = jnp.zeros_like(probe_grad_ref)

    @pl.when(mode == 0)
    def _():
        piece_ref[...] = jnp.zeros_like(piece_ref)

    @pl.when(alive)
    def _():
        weight = (power_ref[0] - measured_ref[0]) / modes
        back = transform(weight * far_ref[0, 0, 0], weight * far_ref[0, 0, 1], left_ref, right_ref, 1)
        term = times_conj((before_ref[0, 0, 0], before_ref[0, 0, 1]), back)
        piece_ref[1, 0] += term[0]
        piece_ref[1, 1] += term[1]
        inner = transform(*times_conj((window_ref[1, 0], window_ref[1, 1]), back), left_ref, right_ref, 0)
        back = transform(*times_conj((prop_ref[0], prop_ref[1]), inner), left_ref, right_ref, 1)
        term = times_conj((probe_ref[mode, 0], probe_ref[mode, 1]), back)
        piece_ref[0, 0] += term[0]
        piece_ref[0, 1] += term[1]
        term = times_conj((window_ref[0, 0], window_ref[0, 1]), back)
        probe_grad_ref[mode, 0] += term[0]
        probe_grad_ref[mode, 1] += term[1]

    @pl.when(alive & (mode == local_modes - 1))
    def _():
        row, col = row_ref[slot], col_ref[slot]
        base = pl.multiple_of(row // 8 * 8, 8)
        extra = row - base
        for layer in range(layers):
            for part in range(2):
                block = piece_ref[layer, part]
                block = jnp.concatenate([block, jnp.zeros((width, columns - width), F32)], axis=1)
                block = pltpu.roll(block, col, 1)
                block = jnp.concatenate([block, jnp.zeros((8, columns), F32)], axis=0)
                block = pltpu.roll(block, extra, 0)
                total_ref[layer, part, pl.ds(base, width + 8), :] += block

    @pl.when((slot == pl.num_programs(0) - 1) & (mode == local_modes - 1))
    def _():
        grad_ref[...] = total_ref[:, :, :tile_rows, :]
        rim_ref[...] = total_ref[:, :, tile_rows:, :]


class Line:
    def __init__(self, own, out_ref, up_ref, down_ref, send_ref, sems):
        self.own, self.out, self.up, self.down, self.send = own, out_ref, up_ref, down_ref, send_ref
        self.sems = sems
        self.n = lax.axis_size("mode")
        self.blocks = out_ref.shape[0]
        place = lax.axis_index("mode")
        left = place < self.n // 2
        self.depth = jnp.where(left, place, self.n - 1 - place)
        self.inward = jnp.where(left, place + 1, place - 1)
        self.outward = jnp.where(left, place - 1, place + 1)
        self.middle = self.depth == self.n // 2 - 1
        self.inner = self.depth > 0

    def copy(self, source, target, sent, received, device, k):
        return pltpu.make_async_remote_copy(
            src_ref=source.at[k], dst_ref=target.at[k],
            send_sem=self.sems.at[sent, k], recv_sem=self.sems.at[received, k],
            device_id={"mode": device}, device_id_type=MESH)

    def in_up(self, k):
        return self.copy(self.send, self.up, 0, 2, self.inward, k)

    def in_across(self, k):
        return self.copy(self.send, self.down, 0, 3, self.inward, k)

    def out_down(self, k):
        return self.copy(self.out, self.down, 1, 3, self.outward, k)

    def greet(self, barrier):
        pl.semaphore_signal(barrier, inc=1, device_id={"mode": self.inward}, device_id_type=MESH)

        @pl.when(self.inner)
        def _():
            pl.semaphore_signal(barrier, inc=1, device_id={"mode": self.outward}, device_id_type=MESH)

        return jnp.where(self.inner, 2, 1)

    def gather(self, k):
        @pl.when(self.inner)
        def _():
            self.in_up(k).wait_recv()
            self.send[k] = self.own(k) + self.up[k]

        @pl.when(jnp.logical_not(self.inner))
        def _():
            self.send[k] = self.own(k)

        @pl.when(self.middle)
        def _():
            self.in_across(k).start()

        @pl.when(jnp.logical_not(self.middle))
        def _():
            self.in_up(k).start()

    def spread(self, k, middle):
        self.in_across(k).wait_recv()
        self.out[k] = self.send[k] + self.down[k] if middle else self.down[k]

        @pl.when(self.inner)
        def _():
            self.out_down(k).start()

    def step(self, t):
        if t < self.blocks:
            self.gather(t)
        if 0 <= t - 1 < self.blocks:
            @pl.when(self.middle)
            def _():
                self.spread(t - 1, True)
        late = t - (self.n - 1)
        if 0 <= late < self.blocks:
            @pl.when(jnp.logical_not(self.middle))
            def _():
                self.spread(late, False)

    def steps(self):
        return self.blocks + self.n - 1

    def drain(self):
        for k in range(self.blocks):
            self.in_up(k).wait_send()

        @pl.when(self.inner)
        def _():
            for k in range(self.blocks):
                self.out_down(k).wait_send()


def mode_sum_kernel(in_ref, out_ref, up_ref, down_ref, send_ref, sems):
    line = Line(lambda k: in_ref[k], out_ref, up_ref, down_ref, send_ref, sems)
    barrier = pltpu.get_barrier_semaphore()
    pl.semaphore_wait(barrier, line.greet(barrier))
    for t in range(line.steps()):
        line.step(t)
    line.drain()


def sum_over_mode(local):
    shape = local.shape
    blocked = local.reshape(BLOCKS, -1, shape[-1])
    buffer = pltpu.VMEM(blocked.shape, F32)
    return pl.pallas_call(
        mode_sum_kernel,
        out_shape=jax.ShapeDtypeStruct(blocked.shape, F32),
        in_specs=[VMEM_SPEC],
        out_specs=VMEM_SPEC,
        scratch_shapes=[buffer, buffer, buffer, pltpu.SemaphoreType.DMA((4, BLOCKS))],
        compiler_params=pltpu.CompilerParams(collective_id=0, has_side_effects=True, vmem_limit_bytes=60 << 20),
        name="mode_sum",
    )(blocked).reshape(shape)


def finish_kernel(grad_ref, rim_ref, probe_ref, out_ref, probe_out_ref,
                  up_ref, down_ref, send_ref, rim_in_ref, part_ref, got_ref, sems, rim_sems, probe_sems):
    tiles = lax.axis_size("tile")
    me = lax.axis_index("tile")
    bits = tiles.bit_length() - 1
    has_next, has_last = me < tiles - 1, me > 0

    def rim_copy(k):
        return pltpu.make_async_remote_copy(
            src_ref=rim_ref.at[k], dst_ref=rim_in_ref.at[k],
            send_sem=rim_sems.at[0, k], recv_sem=rim_sems.at[1, k],
            device_id={"tile": me + 1}, device_id_type=MESH)

    def own(k):
        return send_ref[k]

    line = Line(own, out_ref, up_ref, down_ref, send_ref, sems)

    def other(bit):
        low = lax.rem(me // (1 << bit), 2)
        return me + (1 - 2 * low) * (1 << bit)

    side = lax.rem(me, 2)

    def probe_copy(step, source, target):
        return pltpu.make_async_remote_copy(
            src_ref=source, dst_ref=target,
            send_sem=probe_sems.at[0, step], recv_sem=probe_sems.at[1, step],
            device_id={"tile": other(0 if step == bits else step)}, device_id_type=MESH)

    def exchange(step):
        if step == 0:
            return probe_copy(0, probe_ref.at[1 - side], got_ref.at[0])
        if step < bits:
            return probe_copy(step, part_ref.at[step - 1], got_ref.at[step])
        return probe_copy(step, part_ref.at[bits - 1], probe_out_ref.at[side])

    barrier = pltpu.get_barrier_semaphore()
    count = line.greet(barrier)
    for bit in range(bits):
        pl.semaphore_signal(barrier, inc=1, device_id={"tile": other(bit)}, device_id_type=MESH)

    @pl.when(has_next)
    def _():
        pl.semaphore_signal(barrier, inc=1, device_id={"tile": me + 1}, device_id_type=MESH)

    @pl.when(has_last)
    def _():
        pl.semaphore_signal(barrier, inc=1, device_id={"tile": me - 1}, device_id_type=MESH)

    pl.semaphore_wait(barrier, count + bits + has_next.astype(jnp.int32) + has_last.astype(jnp.int32))

    exchange(0).start()

    @pl.when(has_next)
    def _():
        for k in range(line.blocks):
            rim_copy(k).start()

    for t in range(line.steps()):
        if t < line.blocks:
            @pl.when(has_last)
            def _():
                rim_copy(t).wait_recv()
                send_ref[t] = grad_ref[t] + rim_in_ref[t]

            @pl.when(jnp.logical_not(has_last))
            def _():
                send_ref[t] = grad_ref[t]
        line.step(t)
        bit = (t - 1) // 3
        if t % 3 == 1 and bit < bits:
            exchange(bit).wait_recv()
            part_ref[bit] = (probe_ref[side] if bit == 0 else part_ref[bit - 1]) + got_ref[bit]
            exchange(bit + 1).start()
    probe_out_ref[side] = part_ref[bits - 1]
    exchange(bits).wait_recv()
    for step in range(bits + 1):
        exchange(step).wait_send()
    line.drain()

    @pl.when(has_next)
    def _():
        for k in range(line.blocks):
            rim_copy(k).wait_send()


def finish(grad, rim, grad_probe):
    bits = lax.axis_size("tile").bit_length() - 1
    blocked = (BLOCKS, -1, grad.shape[-1])
    own, edge = grad.reshape(blocked), rim.reshape(blocked)
    halves = grad_probe.reshape(2, -1, grad_probe.shape[-1])
    buffer = pltpu.VMEM(own.shape, F32)
    parts = pltpu.VMEM((bits, *halves.shape[1:]), F32)
    object_grad, probe_grad = pl.pallas_call(
        finish_kernel,
        out_shape=(jax.ShapeDtypeStruct(own.shape, F32), jax.ShapeDtypeStruct(halves.shape, F32)),
        in_specs=[VMEM_SPEC] * 3,
        out_specs=(VMEM_SPEC, VMEM_SPEC),
        scratch_shapes=[buffer, buffer, buffer, buffer, parts, parts,
                        pltpu.SemaphoreType.DMA((4, BLOCKS)), pltpu.SemaphoreType.DMA((2, BLOCKS)),
                        pltpu.SemaphoreType.DMA((2, bits + 1))],
        compiler_params=pltpu.CompilerParams(collective_id=1, has_side_effects=True, vmem_limit_bytes=60 << 20),
        name="finish",
    )(own, edge, halves)
    return object_grad.reshape(grad.shape), probe_grad.reshape(grad_probe.shape)


def per_device(object_field, probe, measured, prop_phase, counts, row_offset, col_offset):
    layers, _, tile_rows, columns = object_field.shape
    width = probe.shape[-1]
    local_modes = probe.shape[0]
    modes = local_modes * lax.axis_size("mode")
    slots = row_offset.shape[0]
    next_rows = shifted(object_field, "tile", -1)
    dft = jnp.asarray(dft_constants(width))
    spectral = jnp.concatenate([jnp.cos(prop_phase)[None], jnp.sin(prop_phase)[None], measured])
    spectral = to_even_odd(spectral)
    prop, measured = spectral[:2], spectral[2:]

    per_mode = pl.BlockSpec((1, 1, 2, width, width), lambda s, m, *_: (s, m, 0, 0, 0))
    per_slot = pl.BlockSpec((1, width, width), lambda s, m, *_: (s, 0, 0))
    ext_shape = pltpu.VMEM((layers, 2, tile_rows + width, columns), F32)
    window_shape = pltpu.VMEM((layers, 2, width, width), F32)
    table_shapes = [pltpu.VMEM((2, 2, width, 3 * width), BF16), pltpu.VMEM((2, 2, 3 * width, width), BF16)]
    per_window = pl.BlockSpec((1, layers, 2, width, width), lambda s, m, *_: (s, 0, 0, 0, 0))
    field = jax.ShapeDtypeStruct((slots, local_modes, 2, width, width), F32)
    params = pltpu.CompilerParams(dimension_semantics=("arbitrary", "arbitrary"), vmem_limit_bytes=60 << 20)

    before, far, local_power, windows = pl.pallas_call(
        forward_kernel,
        out_shape=(field, field, jax.ShapeDtypeStruct((slots, width, width), F32),
                   jax.ShapeDtypeStruct((slots, layers, 2, width, width), F32)),
        grid_spec=pltpu.PrefetchScalarGridSpec(
            num_scalar_prefetch=3,
            grid=(slots, local_modes),
            in_specs=[VMEM_SPEC] * 5,
            out_specs=(per_mode, per_mode, per_slot, per_window),
            scratch_shapes=[ext_shape, *table_shapes],
        ),
        compiler_params=params,
        name="forward",
    )(counts, row_offset, col_offset, object_field, next_rows, probe, prop, dft)

    power = sum_over_mode(local_power)

    whole = lambda shape: pl.BlockSpec(shape, lambda s, m, *_: (0,) * len(shape))
    grad, rim, grad_probe = pl.pallas_call(
        functools.partial(backward_kernel, modes=modes),
        out_shape=(
            jax.ShapeDtypeStruct(object_field.shape, F32),
            jax.ShapeDtypeStruct((layers, 2, width, columns), F32),
            jax.ShapeDtypeStruct(probe.shape, F32),
        ),
        grid_spec=pltpu.PrefetchScalarGridSpec(
            num_scalar_prefetch=3,
            grid=(slots, local_modes),
            in_specs=[VMEM_SPEC] * 3 + [per_mode, per_mode, per_slot, per_slot, per_window],
            out_specs=(whole(object_field.shape), whole((layers, 2, width, columns)), whole(probe.shape)),
            scratch_shapes=[window_shape, ext_shape, *table_shapes],
        ),
        compiler_params=params,
        name="backward",
    )(counts, row_offset, col_offset, probe, prop, dft, before, far, power, measured, windows)

    return finish(grad, rim, grad_probe)


def solution(mesh):
    placed = (
        P(None, None, "tile", None),
        P("mode", None, None, None),
        P("tile", None, None),
        P(),
        P("tile"),
        P("tile"),
        P("tile"),
    )
    return jax.shard_map(
        per_device,
        mesh=mesh,
        in_specs=placed,
        out_specs=(P(None, None, "tile", None), P("mode", None, None, None)),
        check_vma=False,
    )
```

profile of v0, /device:TPU:1, one launch (start us, length us, event | category | flops | bytes accessed | tf_op | source)
XLA Modules:
  0.0 179.3 jit_solution(6048603693775694782)
XLA Ops:
  0.6 1.9 %collective-permute-start = (f32[2,2,256,384]{3,2,1,0:T(8,128)}, f32[2,2,256,384]{3,2,1,0:T(8,128)S(1)}, u32[]{:S(2)}, u32[]{:S(2)}) collective-permute-start(f32[2,2,256,384]{3,2,1,0:T(8,128)} %own_ref.1), channel_id=1, source_target_pairs={{4,0},{8,4},{12,8},{16,12},{20,16},{24,20},{28,24},{5,1},{9,5},{13... | collective-permute-start | bytes 4718600 | tf_op jit(solution)/shard_map/ppermute | solution.py:22
  2.6 1.9 %cosine_bitcast_fusion = (f32[1,256,256]{2,1,0:T(8,128)S(1)}, f32[1,256,256]{2,1,0:T(8,128)S(1)}) fusion(f32[256,256]{1,0:T(8,128)} %param.12), kind=kLoop, calls=%fused_computation.8 | loop fusion | bytes 786432 | tf_op jit(solution)/shard_map/broadcast_in_dim | solution.py:437
  4.4 0.0 copy-start.2
  4.4 2.9 %fusion = f32[6,256,256]{1,2,0:T(8,128)S(1)} fusion(f32[256,256,1]{1,0,2:T(8,128)} %constant.11, f32[4,256,256]{2,1,0:T(8,128)} %param.11, f32[1,256,256]{2,1,0:T(8,128)S(1)} %get-tuple-element.21, f32[1,256,256]{2,1,0:T(8,128)S(1)} %get-tuple-element.20), kind=kOutput, calls=%fused_computation | convolution fusion | flops 1208745984 | bytes 3407872 | tf_op jit(solution)/shard_map/ajk,lk->ajl/dot_general | solution.py:88
  7.3 0.0 copy-done.2
  7.3 1.5 convolution_bitcast_fusion
  8.9 0.8 slice.8.prop_ref
  9.7 1.0 slice.9.measured_ref
  11.4 12.0 %collective-permute-done.next_ref = f32[2,2,256,384]{3,2,1,0:T(8,128)S(1)} collective-permute-done((f32[2,2,256,384]{3,2,1,0:T(8,128)}, f32[2,2,256,384]{3,2,1,0:T(8,128)S(1)}, u32[]{:S(2)}, u32[]{:S(2)}) %collective-permute-start) | collective-permute-done | bytes 1572896 | tf_op jit(solution)/shard_map/ppermute | solution.py:22
  23.4 0.0 copy-start
  23.4 1.1 copy-done
  24.6 14.9 %forward.1 = (f32[4,2,2,256,256]{4,3,2,1,0:T(8,128)}, f32[4,2,2,256,256]{4,3,2,1,0:T(8,128)}, f32[4,256,256]{2,1,0:T(8,128)}, f32[4,2,2,256,256]{4,3,2,1,0:T(8,128)}) custom-call(s32[1]{0:T(128)S(6)} %copy.15.count_ref, s32[4]{0:T(128)} %row_ref.3, s32[4]{0:T(128)} %col_ref.3, f32[2,2,256,384]{3,2,1,0:T(8,128)} %own_ref.1, f32[2,2,256,384]{3,2,1,0:T(8,128)} %copy-done, ...), custom_call_target="tpu_custom_call" | custom-call | tf_op jit(solution)/shard_map/forward/pallas_call | solution.py:450
  39.5 33.1 %mode_sum.1 = f32[8,128,256]{2,1,0:T(8,128)} custom-call(f32[8,128,256]{2,1,0:T(8,128)} %bitcast.22), custom_call_target="tpu_custom_call" | custom-call | tf_op jit(solution)/shard_map/mode_sum/pallas_call | solution.py:310
  72.5 16.6 %backward.1 = (f32[2,2,256,384]{3,2,1,0:T(8,128)}, f32[2,2,256,384]{3,2,1,0:T(8,128)}, f32[2,2,256,256]{3,2,1,0:T(8,128)}) custom-call(s32[1]{0:T(128)S(6)} %copy.15.count_ref, s32[4]{0:T(128)} %row_ref.3, s32[4]{0:T(128)} %col_ref.3, f32[2,2,256,256]{3,2,1,0:T(8,128)} %probe_ref.3, f32[2,256,256]{2,1,0:T(8,128)} %slice.8.prop_ref, ...), custom_call_target="tpu_custom_call" | custom-call | tf_op jit(solution)/shard_map/backward/pallas_call | solution.py:468
  89.1 86.4 %finish.1 = (f32[8,128,384]{2,1,0:T(8,128)}, f32[2,512,256]{2,1,0:T(8,128)}) custom-call(f32[8,128,384]{2,1,0:T(8,128)} %bitcast.19, f32[8,128,384]{2,1,0:T(8,128)} %bitcast.20, f32[2,512,256]{2,1,0:T(8,128)} %bitcast.23), custom_call_target="tpu_custom_call" | custom-call | tf_op jit(solution)/shard_map/finish/pallas_call | solution.py:415
  175.5 0.0 copy-start.1
  175.5 2.7 %copy.16 = f32[2,2,256,384]{3,2,1,0:T(8,128)} copy(f32[2,2,256,384]{3,2,1,0:T(8,128)} %bitcast.18) | data formatting | bytes 3145728
  178.3 0.0 copy-done.1
  178.3 1.0 copy.17
Async XLA Ops:
  0.6 22.8 %collective-permute-start = (f32[2,2,256,384]{3,2,1,0:T(8,128)}, f32[2,2,256,384]{3,2,1,0:T(8,128)S(1)}, u32[]{:S(2)}, u32[]{:S(2)}) collective-permute-start(f32[2,2,256,384]{3,2,1,0:T(8,128)} %own_ref.1), channel_id=1, source_target_pairs={{4,0},{8,4},{12,8},{16,12},{20,16},{24,20},{28,24},{5,1},{9,5},{13... | collective-permute-start | bytes 4718600 | tf_op jit(solution)/shard_map/ppermute | solution.py:22
  4.4 2.9 %copy-start.2 = (f32[256,256,1]{1,0,2:T(8,128)S(1)}, f32[256,256,1]{1,0,2:T(8,128)}, u32[]{:S(2)}) copy-start(f32[256,256,1]{1,0,2:T(8,128)} %constant.11) | copy-start | bytes 786436
  23.4 1.1 copy-start
  175.5 2.8 %copy-start.1 = (f32[2,512,256]{2,1,0:T(8,128)S(1)}, f32[2,512,256]{2,1,0:T(8,128)}, u32[]{:S(2)}) copy-start(f32[2,512,256]{2,1,0:T(8,128)} %get-tuple-element.19) | copy-start | bytes 3145732
where the time goes:
time: 182 us; the launch traced here: 179 us
  Pallas kernels  151 us (83%)
  waiting for transfers between devices  12 us (7%)
  local copies, waits for them, and re-layouts  8.61 us (5%)
  matrix products  4.4 us (2%)
  starting transfers between devices  1.93 us (1%)
    pallas_call x1, Pallas kernels, finish(): pl.pallas_call(finish_kernel, out_shape=(jax.ShapeDtypeStruct(own.shape,...  86.4 us
    pallas_call x1, Pallas kernels, sum_over_mode(): pl.pallas_call(mode_sum_kernel, out_shape=jax.ShapeDtypeStruct(blocked.sh...  33.1 us
    pallas_call x1, Pallas kernels, per_device(): pl.pallas_call(functools.partial(backward_kernel, modes=modes), out_shape...  16.6 us
    pallas_call x1, Pallas kernels, per_device(): pl.pallas_call(forward_kernel, out_shape=(field, field, jax.ShapeDtypeStr...  14.9 us
    ppermute x1, waiting for transfers between devices, shifted(): return lax.ppermute(block, axis, route)  12 us
    unnamed x8, local copies, waits for them, and re-layouts  4.87 us
  transfers between devices with their start and end apart: 1, of which 1 were waited for; matrix products, arithmetic and copies ran while one was open for 5% of the time, Pallas kernels for 0%

commit v1 on v0

--- a/solution.py
+++ b/solution.py
@@ -12,7 +12,7 @@
 F32 = jnp.float32
 BF16 = jnp.bfloat16
 MESH = pl.DeviceIdType.MESH
-BLOCKS = 8
+BLOCKS = 16
 VMEM_SPEC = pl.BlockSpec(memory_space=pltpu.VMEM)
 
 
@@ -271,18 +271,18 @@
     def step(self, t):
         if t < self.blocks:
             self.gather(t)
-        if 0 <= t - 1 < self.blocks:
+        if 0 <= t - 2 < self.blocks:
             @pl.when(self.middle)
             def _():
-                self.spread(t - 1, True)
-        late = t - (self.n - 1)
+                self.spread(t - 2, True)
+        late = t - self.blocks
         if 0 <= late < self.blocks:
             @pl.when(jnp.logical_not(self.middle))
             def _():
                 self.spread(late, False)
 
     def steps(self):
-        return self.blocks + self.n - 1
+        return 2 * self.blocks
 
     def drain(self):
         for k in range(self.blocks):
@@ -388,8 +388,8 @@
             def _():
                 send_ref[t] = grad_ref[t]
         line.step(t)
-        bit = (t - 1) // 3
-        if t % 3 == 1 and bit < bits:
+        bit = 0 if t == 1 else (t - 4) // 5
+        if t == 1 or (t % 5 == 4 and 0 < bit < bits):
             exchange(bit).wait_recv()
             part_ref[bit] = (probe_ref[side] if bit == 0 else part_ref[bit - 1]) + got_ref[bit]
             exchange(bit + 1).start()

time: 182 us -> 164 us (0.901)
  the two profiles are of different devices: /device:TPU:1 before, /device:TPU:0 now
where the time goes in v1:
time: 164 us
  Pallas kernels  148 us (90%)
  local copies, waits for them, and re-layouts  8.6 us (5%)
  matrix products  4.4 us (3%)
    pallas_call x1, Pallas kernels, finish(): pl.pallas_call(finish_kernel, out_shape=(jax.ShapeDtypeStruct(own.shape,...  74.6 us
    pallas_call x1, Pallas kernels, sum_over_mode(): pl.pallas_call(mode_sum_kernel, out_shape=jax.ShapeDtypeStruct(blocked.sh...  34.1 us
    pallas_call x1, Pallas kernels, per_device(): pl.pallas_call(functools.partial(backward_kernel, modes=modes), out_shape...  20.8 us
    pallas_call x1, Pallas kernels, per_device(): pl.pallas_call(forward_kernel, out_shape=(field, field, jax.ShapeDtypeStr...  18.6 us
    unnamed x8, local copies, waits for them, and re-layouts  4.86 us
  transfers between devices with their start and end apart: 1, of which 0 were waited for; matrix products, arithmetic and copies ran while one was open for 5% of the time, Pallas kernels for 0%

profile of v1, /device:TPU:0, one launch (start us, length us, event | category | flops | bytes accessed | tf_op | source)
XLA Modules:
  0.0 163.8 jit_solution(2755811228573350680)
XLA Ops:
  0.6 1.3 collective-permute-start
  1.9 1.9 %cosine_bitcast_fusion = (f32[1,256,256]{2,1,0:T(8,128)S(1)}, f32[1,256,256]{2,1,0:T(8,128)S(1)}) fusion(f32[256,256]{1,0:T(8,128)} %param.12), kind=kLoop, calls=%fused_computation.8 | loop fusion | bytes 786432 | tf_op jit(solution)/shard_map/broadcast_in_dim | solution.py:437
  3.8 0.0 copy-start.2
  3.8 2.8 %fusion = f32[6,256,256]{1,2,0:T(8,128)S(1)} fusion(f32[256,256,1]{1,0,2:T(8,128)} %constant.11, f32[4,256,256]{2,1,0:T(8,128)} %param.11, f32[1,256,256]{2,1,0:T(8,128)S(1)} %get-tuple-element.21, f32[1,256,256]{2,1,0:T(8,128)S(1)} %get-tuple-element.20), kind=kOutput, calls=%fused_computation | convolution fusion | flops 1208745984 | bytes 3407872 | tf_op jit(solution)/shard_map/ajk,lk->ajl/dot_general | solution.py:88
  6.7 0.0 copy-done.2
  6.7 1.5 convolution_bitcast_fusion
  8.2 0.8 slice.8.prop_ref
  9.1 1.0 slice.9.measured_ref
  10.8 0.0 collective-permute-done.next_ref
  10.8 0.0 copy-start
  10.8 1.1 copy-done
  11.9 18.6 %forward.1 = (f32[4,2,2,256,256]{4,3,2,1,0:T(8,128)}, f32[4,2,2,256,256]{4,3,2,1,0:T(8,128)}, f32[4,256,256]{2,1,0:T(8,128)}, f32[4,2,2,256,256]{4,3,2,1,0:T(8,128)}) custom-call(s32[1]{0:T(128)S(6)} %copy.15.count_ref, s32[4]{0:T(128)} %row_ref.3, s32[4]{0:T(128)} %col_ref.3, f32[2,2,256,384]{3,2,1,0:T(8,128)} %own_ref.1, f32[2,2,256,384]{3,2,1,0:T(8,128)} %copy-done, ...), custom_call_target="tpu_custom_call" | custom-call | tf_op jit(solution)/shard_map/forward/pallas_call | solution.py:450
  30.5 34.1 %mode_sum.1 = f32[16,64,256]{2,1,0:T(8,128)} custom-call(f32[16,64,256]{2,1,0:T(8,128)} %bitcast.22), custom_call_target="tpu_custom_call" | custom-call | tf_op jit(solution)/shard_map/mode_sum/pallas_call | solution.py:310
  64.6 20.8 %backward.1 = (f32[2,2,256,384]{3,2,1,0:T(8,128)}, f32[2,2,256,384]{3,2,1,0:T(8,128)}, f32[2,2,256,256]{3,2,1,0:T(8,128)}) custom-call(s32[1]{0:T(128)S(6)} %copy.15.count_ref, s32[4]{0:T(128)} %row_ref.3, s32[4]{0:T(128)} %col_ref.3, f32[2,2,256,256]{3,2,1,0:T(8,128)} %probe_ref.3, f32[2,256,256]{2,1,0:T(8,128)} %slice.8.prop_ref, ...), custom_call_target="tpu_custom_call" | custom-call | tf_op jit(solution)/shard_map/backward/pallas_call | solution.py:468
  85.4 74.6 %finish.1 = (f32[16,64,384]{2,1,0:T(8,128)}, f32[2,512,256]{2,1,0:T(8,128)}) custom-call(f32[16,64,384]{2,1,0:T(8,128)} %bitcast.19, f32[16,64,384]{2,1,0:T(8,128)} %bitcast.20, f32[2,512,256]{2,1,0:T(8,128)} %bitcast.23), custom_call_target="tpu_custom_call" | custom-call | tf_op jit(solution)/shard_map/finish/pallas_call | solution.py:415
  160.1 0.0 copy-start.1
  160.1 2.7 %copy.16 = f32[2,2,256,384]{3,2,1,0:T(8,128)} copy(f32[2,2,256,384]{3,2,1,0:T(8,128)} %bitcast.18) | data formatting | bytes 3145728
  162.8 0.0 copy-done.1
  162.8 1.0 copy.17
Async XLA Ops:
  0.6 10.1 %collective-permute-start = (f32[2,2,256,384]{3,2,1,0:T(8,128)}, f32[2,2,256,384]{3,2,1,0:T(8,128)S(1)}, u32[]{:S(2)}, u32[]{:S(2)}) collective-permute-start(f32[2,2,256,384]{3,2,1,0:T(8,128)} %own_ref.1), channel_id=1, source_target_pairs={{4,0},{8,4},{12,8},{16,12},{20,16},{24,20},{28,24},{5,1},{9,5},{13... | collective-permute-start | bytes 4718600 | tf_op jit(solution)/shard_map/ppermute | solution.py:22
  3.8 2.9 %copy-start.2 = (f32[256,256,1]{1,0,2:T(8,128)S(1)}, f32[256,256,1]{1,0,2:T(8,128)}, u32[]{:S(2)}) copy-start(f32[256,256,1]{1,0,2:T(8,128)} %constant.11) | copy-start | bytes 786436
  10.8 1.1 copy-start
  160.1 2.8 %copy-start.1 = (f32[2,512,256]{2,1,0:T(8,128)S(1)}, f32[2,512,256]{2,1,0:T(8,128)}, u32[]{:S(2)}) copy-start(f32[2,512,256]{2,1,0:T(8,128)} %get-tuple-element.19) | copy-start | bytes 3145732
